TPU v7x, 256 devices: a whole 4x4x8 slice. The times are simulated.
256 devices in a mesh: occ: 32 (over z, x_hi, core), vir: 8 (over x_lo, y).
Axes of the slice: x: 4 (x_hi: 2, x_lo: 2; x = x_hi * 2 + x_lo), y: 4, z: 8, core: 2. Of those that a mesh axis runs over, the one named last changes fastest.
Arguments:
- factors: bfloat16 [32, 1024, 3072], P('occ', 'vir'), may hold values from -0.71875 to 0.71875
- occ_energy: float32 [32], replicated, may hold values from -2 to -0.4
- vir_energy: float32 [1024], replicated, may hold values from 0.4 to 4
- density_in: float32 [32, 1024, 3072], P('occ', 'vir'), may hold values from -3 to 3
Outputs:
- density: float32 [32, 1024, 3072], P('occ', 'vir')
All inputs are finite; a program needn't handle non-finite values.
Results may differ from a plain program's by a relative error of at most 0.0027.
Values may be sent and summed in bfloat16 or wider, within the bound.
No kernel may reach another device: no remote copies, remote signals or barrier semaphores. Data moves between devices by JAX's collectives and lax.ppermute only.
A program may use at most 128 MiB of HBM per device.

v0:
```python
import jax
import jax.numpy as jnp
from jax import lax
from jax.sharding import PartitionSpec as P

VISITS = 3


def passed_along(block, axis, distance):
    devices = range(lax.axis_size(axis))
    route = [((i - distance) % len(devices), i) for i in devices]
    return lax.ppermute(block, axis, route)


def on_device(factors, occ_energy, vir_energy, density_in):
    occ_rows = factors.shape[0]
    vir_local = factors.shape[1]
    aux_width = factors.shape[2]
    vir_whole = vir_energy.shape[0]
    occ_rank = lax.axis_index("occ")
    cycle_size = lax.axis_size("occ")
    vir_rank = lax.axis_index("vir")
    e_own = lax.dynamic_slice_in_dim(occ_energy, occ_rank * occ_rows, occ_rows, 0)
    e_local = lax.dynamic_slice_in_dim(vir_energy, vir_rank * vir_local, vir_local, 0)
    flat_own = factors.reshape(occ_rows * vir_local, aux_width)
    total = density_in.reshape(occ_rows * vir_local, aux_width)
    partner_shard = factors
    partner = factors
    for visit in range(VISITS):
        if visit > 0:
            partner_shard = passed_along(partner_shard, "occ", 1)
        partner = lax.all_gather(partner_shard, "vir", axis=1, tiled=True)
        other = (occ_rank - visit) % cycle_size * occ_rows
        e_partner = lax.dynamic_slice_in_dim(occ_energy, other, occ_rows, 0)
        flat_partner = partner.reshape(occ_rows * vir_whole, aux_width)
        direct = lax.dot_general(
            flat_own, flat_partner, (((1,), (1,)), ((), ())), preferred_element_type=jnp.float32
        )
        direct = direct.astype(jnp.bfloat16).reshape(occ_rows, vir_local, occ_rows, vir_whole)
        swapped = lax.all_to_all(direct, "vir", split_axis=3, concat_axis=1, tiled=True).transpose(
            0, 3, 2, 1
        )
        denom = (
            e_own[:, None, None, None]
            + e_partner[None, None, :, None]
            - e_local[None, :, None, None]
            - vir_energy[None, None, None, :]
        )
        amp = ((2.0 * direct.astype(jnp.float32) - swapped.astype(jnp.float32)) / denom).astype(
            jnp.bfloat16
        )
        total = total + jnp.dot(
            amp.reshape(occ_rows * vir_local, occ_rows * vir_whole),
            flat_partner,
            preferred_element_type=jnp.float32,
        )
    return total.reshape(density_in.shape)


def solution(mesh):
    return jax.shard_map(
        on_device,
        mesh=mesh,
        in_specs=(P("occ", "vir", None), P(), P(), P("occ", "vir", None)),
        out_specs=P("occ", "vir", None),
        check_vma=False,
    )
```

profile of v0, /device:TPU:4, one launch (start us, length us, event | category | flops | bytes accessed | tf_op | source)
XLA Modules:
  0.0 283.8 jit_solution(7729517185686654184)
XLA Ops:
  6.5 0.0 copy-start.4
  6.5 0.0 copy-start.3
  6.5 0.0 all-gather.4.cloned.1.call-start
  6.5 0.7 all-gather.4.cloned.1.call-update
  7.3 0.0 all-gather.6.cloned.1.call-start
  7.3 0.1 collective-permute-start
  7.4 13.1 %collective-permute-done = bf16[1,128,3072]{2,1,0:T(8,128)(2,1)S(1)} collective-permute-done((bf16[1,128,3072]{2,1,0:T(8,128)(2,1)}, bf16[1,128,3072]{2,1,0:T(8,128)(2,1)S(1)}, u32[]{:S(2)}, u32[]{:S(2)}) %collective-permute-start) | collective-permute-done | bytes 786464 | tf_op jit(solution)/shard_map/ppermute | solution.py:12
  20.5 0.0 copy-start.2
  20.5 0.9 copy-done.2
  21.4 0.0 all-gather.6.cloned.1.call-update
  21.4 0.0 all-gather.8.cloned.1.call-start
  21.5 0.1 collective-permute-start.1
  21.6 29.9 %collective-permute-done.1 = bf16[1,128,3072]{2,1,0:T(8,128)(2,1)S(1)} collective-permute-done((bf16[1,128,3072]{2,1,0:T(8,128)(2,1)}, bf16[1,128,3072]{2,1,0:T(8,128)(2,1)S(1)}, u32[]{:S(2)}, u32[]{:S(2)}) %collective-permute-start.1) | collective-permute-done | bytes 786464 | tf_op jit(solution)/shard_map/ppermute | solution.py:12
  51.4 0.0 copy-start.1
  51.4 0.9 copy-done.1
  52.3 0.0 all-gather.8.cloned.1.call-update
  52.3 0.0 copy-start
  52.3 42.7 %all-gather.4.cloned.1.call-done = bf16[1,1024,3072]{2,1,0:T(8,128)(2,1)} async-done(((bf16[1,128,3072]{2,1,0:T(8,128)(2,1)}), bf16[1,1024,3072]{2,1,0:T(8,128)(2,1)}) %all-gather.4.cloned.1.call-update) | async-done | bytes 6291472 | tf_op jit(solution)/shard_map/all_gather | solution.py:32
  95.1 5.3 %fusion.24 = bf16[128,1024]{1,0:T(8,128)(2,1)S(1)} fusion(bf16[1,1024,3072]{2,1,0:T(8,128)(2,1)} %all-gather.4.cloned.1.call-done, bf16[1,128,3072]{2,1,0:T(8,128)(2,1)} %param.4), kind=kOutput, calls=%fused_computation.16 | convolution fusion | flops 805437440 | bytes 7340032 | tf_op jit(solution)/shard_map/dot_general | solution.py:36
  100.3 0.4 copy.8
  100.7 0.6 broadcast.152
  101.3 2.2 reduce
  103.6 0.8 reshape.223
  104.4 3.4 %all-to-all-start = ((bf16[8,2,8192]{2,1,0:T(2,128)(2,1)}), bf16[8,2,8192]{2,1,0:T(2,128)(2,1)S(1)}, u32[]{:S(2)}, u32[]{:S(2)}) async-start(bf16[8,2,8192]{2,1,0:T(2,128)(2,1)} %reshape.223), calls=%async_computation | async-start | bytes 524288 | tf_op jit(solution)/shard_map/all_to_all | solution.py:40
  107.8 0.0 copy-done.4
  107.8 0.7 fusion.57
  112.2 0.0 copy-done.3
  112.2 0.1 broadcast_subtract_fusion
  112.3 6.5 %all-to-all-done = bf16[8,2,8192]{2,1,0:T(2,128)(2,1)S(1)} async-done(((bf16[8,2,8192]{2,1,0:T(2,128)(2,1)}), bf16[8,2,8192]{2,1,0:T(2,128)(2,1)S(1)}, u32[]{:S(2)}, u32[]{:S(2)}) %all-to-all-start) | async-done | bytes 262176 | tf_op jit(solution)/shard_map/all_to_all | solution.py:40
  118.8 0.3 reshape.224
  119.0 0.5 bitcast_convert_fusion.2
  119.6 0.3 copy.19
  119.9 0.1 reshape.217
  120.0 53.0 %all-gather.6.cloned.1.call-done = bf16[1,1024,3072]{2,1,0:T(8,128)(2,1)} async-done(((bf16[1,128,3072]{2,1,0:T(8,128)(2,1)}), bf16[1,1024,3072]{2,1,0:T(8,128)(2,1)}) %all-gather.6.cloned.1.call-update) | async-done | bytes 6291472 | tf_op jit(solution)/shard_map/all_gather | solution.py:32
  173.0 0.0 copy-done
  173.0 5.0 %fusion.27 = bf16[128,1024]{1,0:T(8,128)(2,1)S(1)} fusion(bf16[1,1024,3072]{2,1,0:T(8,128)(2,1)} %all-gather.6.cloned.1.call-done, bf16[1,128,3072]{2,1,0:T(8,128)(2,1)S(1)} %copy-done), kind=kOutput, calls=%fused_computation.17 | convolution fusion | flops 805437440 | bytes 7340032 | tf_op jit(solution)/shard_map/dot_general | solution.py:36
  178.0 0.4 copy.10
  178.4 2.3 reduce.1
  180.7 0.8 reshape.225
  181.5 4.2 %all-to-all-start.1 = ((bf16[8,2,8192]{2,1,0:T(2,128)(2,1)}), bf16[8,2,8192]{2,1,0:T(2,128)(2,1)}, u32[]{:S(2)}, u32[]{:S(2)}) async-start(bf16[8,2,8192]{2,1,0:T(2,128)(2,1)} %reshape.225), calls=%async_computation.1 | async-start | bytes 524288 | tf_op jit(solution)/shard_map/all_to_all | solution.py:40
  185.7 4.4 %fusion.12 = f32[128,3072]{1,0:T(8,128)S(1)} fusion(bf16[1,1024,3072]{2,1,0:T(8,128)(2,1)} %all-gather.4.cloned.1.call-done, f32[1,128,3072]{2,1,0:T(8,128)} %param.7, f32[1,1024,1,128]{1,3,2,0:T(8,128)S(1)} %reshape.217, bf16[128,1024]{1,0:T(8,128)(2,1)S(1)} %fusion.24, f32[1024]{0:T(1024)S(1)} %copy-done.3, f32[128]{0:T(128)S(1)} %get-tuple-element.7), kind=kOutput, calls=%fused_computation.12 | convolution fusion | flops 806486016 | bytes 10228224 | tf_op jit(solution)/shard_map/dot_general | solution.py:52
  190.1 6.5 %all-to-all-done.1 = bf16[8,2,8192]{2,1,0:T(2,128)(2,1)} async-done(((bf16[8,2,8192]{2,1,0:T(2,128)(2,1)}), bf16[8,2,8192]{2,1,0:T(2,128)(2,1)}, u32[]{:S(2)}, u32[]{:S(2)}) %all-to-all-start.1) | async-done | bytes 262176 | tf_op jit(solution)/shard_map/all_to_all | solution.py:40
  196.5 1.2 reshape.226
  197.7 0.5 bitcast_convert_fusion.1
  198.3 1.1 copy.18
  199.4 1.1 reshape.218
  200.5 50.8 %all-gather.8.cloned.1.call-done = bf16[1,1024,3072]{2,1,0:T(8,128)(2,1)} async-done(((bf16[1,128,3072]{2,1,0:T(8,128)(2,1)}), bf16[1,1024,3072]{2,1,0:T(8,128)(2,1)}) %all-gather.8.cloned.1.call-update) | async-done | bytes 6291472 | tf_op jit(solution)/shard_map/all_gather | solution.py:32
  251.3 5.0 %fusion.30 = bf16[128,1024]{1,0:T(8,128)(2,1)S(1)} fusion(bf16[1,1024,3072]{2,1,0:T(8,128)(2,1)} %all-gather.8.cloned.1.call-done, bf16[1,128,3072]{2,1,0:T(8,128)(2,1)S(1)} %copy-done), kind=kOutput, calls=%fused_computation.18 | convolution fusion | flops 805437440 | bytes 7340032 | tf_op jit(solution)/shard_map/dot_general | solution.py:36
  256.3 0.4 copy.12
  256.7 2.3 reduce.2
  258.9 0.8 reshape.227
  259.7 3.4 %all-to-all-start.2 = ((bf16[8,2,8192]{2,1,0:T(2,128)(2,1)}), bf16[8,2,8192]{2,1,0:T(2,128)(2,1)S(1)}, u32[]{:S(2)}, u32[]{:S(2)}) async-start(bf16[8,2,8192]{2,1,0:T(2,128)(2,1)} %reshape.227), calls=%async_computation.2 | async-start | bytes 524288 | tf_op jit(solution)/shard_map/all_to_all | solution.py:40
  263.1 5.0 %fusion.15 = f32[128,3072]{1,0:T(8,128)} fusion(f32[128,3072]{1,0:T(8,128)S(1)} %fusion.12, bf16[1,1024,3072]{2,1,0:T(8,128)(2,1)} %all-gather.6.cloned.1.call-done, f32[1,1024,1,128]{1,3,2,0:T(8,128)S(1)} %reshape.218, bf16[128,1024]{1,0:T(8,128)(2,1)S(1)} %fusion.27, f32[128]{0:T(128)S(1)} %get-tuple-element.6, f32[1024]{0:T(1024)S(1)} %copy-done.3), kind=kOutput, calls=%fused_computation.13 | convolution fusion | flops 806486016 | bytes 10228224 | tf_op jit(solution)/shard_map/dot_general | solution.py:52
  268.2 2.4 all-to-all-done.2
  270.6 0.3 reshape.228
  270.8 0.5 bitcast_convert_fusion
  271.4 0.3 copy.17
  271.7 0.1 reshape.219
  271.8 5.5 %fusion.21 = f32[1,128,3072]{2,1,0:T(8,128)} fusion(f32[128,3072]{1,0:T(8,128)} %fusion.15, bf16[1,1024,3072]{2,1,0:T(8,128)(2,1)} %all-gather.8.cloned.1.call-done, f32[1,1024,1,128]{1,3,2,0:T(8,128)S(1)} %reshape.219, bf16[128,1024]{1,0:T(8,128)(2,1)S(1)} %fusion.30, f32[128]{0:T(128)S(1)} %get-tuple-element.5, f32[1024]{0:T(1024)S(1)} %copy-done.3), kind=kOutput, calls=%fused_computation.15 | convolution fusion | flops 806486016 | bytes 10228224 | tf_op jit(solution)/shard_map/dot_general | solution.py:52
Async XLA Ops:
  6.5 101.3 %copy-start.4 = (f32[32]{0:T(128)S(1)}, f32[32]{0:T(128)}, u32[]{:S(2)}) copy-start(f32[32]{0:T(128)} %param.5) | copy-start | bytes 388
  6.5 105.7 %copy-start.3 = (f32[1024]{0:T(1024)S(1)}, f32[1024]{0:T(1024)}, u32[]{:S(2)}) copy-start(f32[1024]{0:T(1024)} %param.6) | copy-start | bytes 12292
  6.5 88.5 %all-gather.4.cloned.1.call-start = ((), (), s32[]{:S(2)}) async-start(), calls=%async_computation.3 | async-start | bytes 7077888 | tf_op jit(solution)/shard_map/all_gather | solution.py:32
  7.3 165.8 %all-gather.6.cloned.1.call-start = ((), (), s32[]{:S(2)}) async-start(), calls=%async_computation.4 | async-start | bytes 7077888 | tf_op jit(solution)/shard_map/all_gather | solution.py:32
  7.3 13.2 %collective-permute-start = (bf16[1,128,3072]{2,1,0:T(8,128)(2,1)}, bf16[1,128,3072]{2,1,0:T(8,128)(2,1)S(1)}, u32[]{:S(2)}, u32[]{:S(2)}) collective-permute-start(bf16[1,128,3072]{2,1,0:T(8,128)(2,1)} %param.4), channel_id=1, source_target_pairs={{248,0},{0,8},{8,16},{16,24},{24,32},{32,40},{40,48},{48,56},{56,6... | collective-permute-start | bytes 2359304 | tf_op jit(solution)/shard_map/ppermute | solution.py:12
  20.5 0.9 copy-start.2
  21.4 229.9 %all-gather.8.cloned.1.call-start = ((), (), s32[]{:S(2)}) async-start(), calls=%async_computation.5 | async-start | bytes 7077888 | tf_op jit(solution)/shard_map/all_gather | solution.py:32
  21.5 29.9 %collective-permute-start.1 = (bf16[1,128,3072]{2,1,0:T(8,128)(2,1)}, bf16[1,128,3072]{2,1,0:T(8,128)(2,1)S(1)}, u32[]{:S(2)}, u32[]{:S(2)}) collective-permute-start(bf16[1,128,3072]{2,1,0:T(8,128)(2,1)} %copy-done.2), channel_id=1, source_target_pairs={{248,0},{0,8},{8,16},{16,24},{24,32},{32,40},{40,48},{48,56},{56,6... | collective-permute-start | bytes 2359304 | tf_op jit(solution)/shard_map/ppermute | solution.py:12
  51.4 0.9 copy-start.1
  52.3 120.7 %copy-start = (bf16[1,128,3072]{2,1,0:T(8,128)(2,1)S(1)}, bf16[1,128,3072]{2,1,0:T(8,128)(2,1)}, u32[]{:S(2)}) copy-start(bf16[1,128,3072]{2,1,0:T(8,128)(2,1)} %param.4) | copy-start | bytes 2359300
  104.4 14.4 %all-to-all-start = ((bf16[8,2,8192]{2,1,0:T(2,128)(2,1)}), bf16[8,2,8192]{2,1,0:T(2,128)(2,1)S(1)}, u32[]{:S(2)}, u32[]{:S(2)}) async-start(bf16[8,2,8192]{2,1,0:T(2,128)(2,1)} %reshape.223), calls=%async_computation | async-start | bytes 524288 | tf_op jit(solution)/shard_map/all_to_all | solution.py:40
  181.5 15.1 %all-to-all-start.1 = ((bf16[8,2,8192]{2,1,0:T(2,128)(2,1)}), bf16[8,2,8192]{2,1,0:T(2,128)(2,1)}, u32[]{:S(2)}, u32[]{:S(2)}) async-start(bf16[8,2,8192]{2,1,0:T(2,128)(2,1)} %reshape.225), calls=%async_computation.1 | async-start | bytes 524288 | tf_op jit(solution)/shard_map/all_to_all | solution.py:40
  259.7 10.8 %all-to-all-start.2 = ((bf16[8,2,8192]{2,1,0:T(2,128)(2,1)}), bf16[8,2,8192]{2,1,0:T(2,128)(2,1)S(1)}, u32[]{:S(2)}, u32[]{:S(2)}) async-start(bf16[8,2,8192]{2,1,0:T(2,128)(2,1)} %reshape.227), calls=%async_computation.2 | async-start | bytes 524288 | tf_op jit(solution)/shard_map/all_to_all | solution.py:40
Sparse Core Ops, SparseCore 0:
  9.1 85.8 all-gather.3
  96.8 76.1 all-gather.5
  174.8 76.4 all-gather.7
where the time goes:
time: 284 us
  waiting for transfers between devices  206 us (73%)
  matrix products  30.1 us (11%)
  between operations  17.1 us (6%)
  local copies, waits for them, and re-layouts  11.3 us (4%)
  starting transfers between devices  11.3 us (4%)
  other arithmetic  8.46 us (3%)
    all_gather x3, waiting for transfers between devices, on_device(): partner = lax.all_gather(partner_shard, 'vir', axis=1, tiled=True)  147 us
    ppermute x2, waiting for transfers between devices, passed_along(): return lax.ppermute(block, axis, route)  43 us
    all_to_all x3, waiting for transfers between devices, on_device(): lax.all_to_all(direct, 'vir', split_axis=3, concat_axis=1, tiled=True)  15.3 us
    dot_general x3, matrix products, on_device(): lax.dot_general(flat_own, flat_partner, (((1,), (1,)), ((), ())), preferr...  15.2 us
    dot_general x3, matrix products, on_device(): jnp.dot(amp.reshape(occ_rows * vir_local, occ_rows * vir_whole), flat_par...  14.9 us
    all_to_all x3, starting transfers between devices, on_device(): lax.all_to_all(direct, 'vir', split_axis=3, concat_axis=1, tiled=True)  11 us
    unnamed x3, other arithmetic  6.75 us
    unnamed x17, local copies, waits for them, and re-layouts  6.4 us
  transfers between devices with their start and end apart: 8, of which 8 were waited for; matrix products, arithmetic and copies ran while one was open for 12% of the time, Pallas kernels for 0%

commit v1 on v0

--- a/solution.py
+++ b/solution.py
@@ -29,7 +29,10 @@
     for visit in range(VISITS):
         if visit > 0:
             partner_shard = passed_along(partner_shard, "occ", 1)
-        partner = lax.all_gather(partner_shard, "vir", axis=1, tiled=True)
+        n_dev = lax.axis_size("vir")
+        blocks = jnp.stack([partner_shard for _ in range(n_dev)])
+        blocks = lax.all_to_all(blocks, "vir", split_axis=0, concat_axis=0)
+        partner = jnp.concatenate(blocks, axis=1)
         other = (occ_rank - visit) % cycle_size * occ_rows
         e_partner = lax.dynamic_slice_in_dim(occ_energy, other, occ_rows, 0)
         flat_partner = partner.reshape(occ_rows * vir_whole, aux_width)

time: 284 us -> 305 us (1.074)
  starting transfers between devices: 11.3 us -> 29.1 us
  between operations: 17.1 us -> 3.74 us
  local copies, waits for them, and re-layouts: 11.3 us -> 22 us
    all_gather x3 -> x0, waiting for transfers between devices: 147 us -> none  [on_device(): partner = lax.all_gather(partner_shard, 'vir', axis=1, tiled=True)]
    all_to_all x0 -> x3, waiting for transfers between devices: none -> 122 us  [on_device(): blocks = lax.all_to_all(blocks, 'vir', split_axis=0, concat_axis=0)]
    ppermute x2, waiting for transfers between devices: 43 us -> 77.2 us  [passed_along(): return lax.ppermute(block, axis, route)]
    all_to_all x0 -> x3, starting transfers between devices: none -> 15.4 us  [on_device(): blocks = lax.all_to_all(blocks, 'vir', split_axis=0, concat_axis=0)]
    another operation x0 -> x3, local copies, waits for them, and re-layouts: none -> 12.7 us  [on_device(): blocks = jnp.stack([partner_shard for _ in range(n_dev)])]
    all_to_all x3, waiting for transfers between devices: 15.3 us -> 9.58 us  [on_device(): lax.all_to_all(direct, 'vir', split_axis=3, concat_axis=1, tiled=True)]
    unnamed x17 -> x15, local copies, waits for them, and re-layouts: 6.4 us -> 4.52 us
  transfers between devices with their start and end apart: 8 -> 8, of which waited for: 8 -> 6; matrix products, arithmetic and copies ran while one was open for 12% -> 11% of each run, Pallas kernels for 0% -> 0%
where the time goes in v1:
time: 305 us; the launch traced here: 302 us
  waiting for transfers between devices  209 us (69%)
  matrix products  29.8 us (10%)
  starting transfers between devices  29.1 us (10%)
  local copies, waits for them, and re-layouts  22 us (7%)
  other arithmetic  8.24 us (3%)
  between operations  3.74 us (1%)
    all_to_all x3, waiting for transfers between devices, on_device(): blocks = lax.all_to_all(blocks, 'vir', split_axis=0, concat_axis=0)  122 us
    ppermute x2, waiting for transfers between devices, passed_along(): return lax.ppermute(block, axis, route)  77.2 us
    all_to_all x3, starting transfers between devices, on_device(): blocks = lax.all_to_all(blocks, 'vir', split_axis=0, concat_axis=0)  15.4 us
    dot_general x3, matrix products, on_device(): lax.dot_general(flat_own, flat_partner, (((1,), (1,)), ((), ())), preferr...  14.9 us
    dot_general x3, matrix products, on_device(): jnp.dot(amp.reshape(occ_rows * vir_local, occ_rows * vir_whole), flat_par...  14.9 us
    all_to_all x3, starting transfers between devices, on_device(): lax.all_to_all(direct, 'vir', split_axis=3, concat_axis=1, tiled=True)  13.6 us
    another operation x3, local copies, waits for them, and re-layouts, on_device(): blocks = jnp.stack([partner_shard for _ in range(n_dev)])  12.7 us
    all_to_all x3, waiting for transfers between devices, on_device(): lax.all_to_all(direct, 'vir', split_axis=3, concat_axis=1, tiled=True)  9.58 us
  transfers between devices with their start and end apart: 8, of which 6 were waited for; matrix products, arithmetic and copies ran while one was open for 11% of the time, Pallas kernels for 0%

profile of v1, /device:TPU:4, one launch (start us, length us, event | category | flops | bytes accessed | tf_op | source)
XLA Modules:
  0.0 302.1 jit_solution(9908088125168099960)
XLA Ops:
  0.0 4.6 %stack.6 = bf16[8,1,128,3072]{3,2,1,0:T(8,128)(2,1)} broadcast(bf16[128,3072]{1,0:T(8,128)(2,1)} %bitcast.112), dimensions={2,3} | broadcast | bytes 7077888 | tf_op jit(solution)/shard_map/stack | solution.py:33
  4.6 0.0 copy-start
  4.6 5.2 %all-to-all-start = ((bf16[8,1,128,3072]{3,2,1,0:T(8,128)(2,1)}), bf16[8,1,128,3072]{3,2,1,0:T(8,128)(2,1)}, u32[]{:S(2)}, u32[]{:S(2)}) async-start(bf16[8,1,128,3072]{3,2,1,0:T(8,128)(2,1)} %stack.6), calls=%async_computation | async-start | bytes 12582912 | tf_op jit(solution)/shard_map/all_to_all | solution.py:34
  9.9 0.0 copy-done
  9.9 0.1 collective-permute-start
  10.0 77.2 %collective-permute-done = bf16[1,128,3072]{2,1,0:T(8,128)(2,1)S(1)} collective-permute-done((bf16[1,128,3072]{2,1,0:T(8,128)(2,1)S(1)}, bf16[1,128,3072]{2,1,0:T(8,128)(2,1)S(1)}, u32[]{:S(2)}, u32[]{:S(2)}) %collective-permute-start) | collective-permute-done | bytes 786464 | tf_op jit(solution)/shard_map/ppermute | solution.py:12
  87.2 1.1 all-to-all-done
  88.3 3.4 %stack.7 = bf16[8,1,128,3072]{3,2,1,0:T(8,128)(2,1)} broadcast(bf16[128,3072]{1,0:T(8,128)(2,1)S(1)} %bitcast.125), dimensions={2,3} | broadcast | bytes 7077888 | tf_op jit(solution)/shard_map/stack | solution.py:33
  91.7 5.0 %all-to-all-start.2 = ((bf16[8,1,128,3072]{3,2,1,0:T(8,128)(2,1)}), bf16[8,1,128,3072]{3,2,1,0:T(8,128)(2,1)}, u32[]{:S(2)}, u32[]{:S(2)}) async-start(bf16[8,1,128,3072]{3,2,1,0:T(8,128)(2,1)} %stack.7), calls=%async_computation.2 | async-start | bytes 12582912 | tf_op jit(solution)/shard_map/all_to_all | solution.py:34
  96.7 0.0 collective-permute-start.1
  96.7 5.0 %convolution_convert_fusion.2 = bf16[128,1024]{1,0:T(8,128)(2,1)S(1)} fusion(bf16[1024,3072]{1,0:T(8,128)(2,1)} %bitcast.2, bf16[1,128,3072]{2,1,0:T(8,128)(2,1)S(1)} %copy-done), kind=kOutput, calls=%fused_computation.6 | convolution fusion | flops 805437440 | bytes 7340032 | tf_op jit(solution)/shard_map/dot_general | solution.py:39
  101.7 0.4 copy.8
  102.1 0.5 broadcast.161
  102.6 2.2 reduce
  104.8 0.8 reshape.220
  105.6 68.3 %all-to-all-done.2 = bf16[8,1,128,3072]{3,2,1,0:T(8,128)(2,1)} async-done(((bf16[8,1,128,3072]{3,2,1,0:T(8,128)(2,1)}), bf16[8,1,128,3072]{3,2,1,0:T(8,128)(2,1)}, u32[]{:S(2)}, u32[]{:S(2)}) %all-to-all-start.2) | async-done | bytes 6291488 | tf_op jit(solution)/shard_map/all_to_all | solution.py:34
  173.9 4.3 %all-to-all-start.1 = ((bf16[8,2,8192]{2,1,0:T(2,128)(2,1)}), bf16[8,2,8192]{2,1,0:T(2,128)(2,1)S(1)}, u32[]{:S(2)}, u32[]{:S(2)}) async-start(bf16[8,2,8192]{2,1,0:T(2,128)(2,1)} %reshape.220), calls=%async_computation.1 | async-start | bytes 524288 | tf_op jit(solution)/shard_map/all_to_all | solution.py:43
  178.2 5.0 %convolution_convert_fusion.1 = bf16[128,1024]{1,0:T(8,128)(2,1)S(1)} fusion(bf16[1024,3072]{1,0:T(8,128)(2,1)} %bitcast.11, bf16[1,128,3072]{2,1,0:T(8,128)(2,1)S(1)} %copy-done), kind=kOutput, calls=%fused_computation.5 | convolution fusion | flops 805437440 | bytes 7340032 | tf_op jit(solution)/shard_map/dot_general | solution.py:39
  183.2 0.4 copy.10
  183.6 2.2 reduce.1
  185.8 0.8 reshape.222
  186.5 0.0 all-to-all-done.1
  186.5 5.7 %all-to-all-start.3 = ((bf16[8,2,8192]{2,1,0:T(2,128)(2,1)}), bf16[8,2,8192]{2,1,0:T(2,128)(2,1)S(1)}, u32[]{:S(2)}, u32[]{:S(2)}) async-start(bf16[8,2,8192]{2,1,0:T(2,128)(2,1)} %reshape.222), calls=%async_computation.3 | async-start | bytes 524288 | tf_op jit(solution)/shard_map/all_to_all | solution.py:43
  192.3 0.0 collective-permute-done.1
  192.3 7.2 %all-to-all-done.3 = bf16[8,2,8192]{2,1,0:T(2,128)(2,1)S(1)} async-done(((bf16[8,2,8192]{2,1,0:T(2,128)(2,1)}), bf16[8,2,8192]{2,1,0:T(2,128)(2,1)S(1)}, u32[]{:S(2)}, u32[]{:S(2)}) %all-to-all-start.3) | async-done | bytes 262176 | tf_op jit(solution)/shard_map/all_to_all | solution.py:43
  199.5 0.0 copy-start.1
  199.5 4.7 %stack.8 = bf16[8,1,128,3072]{3,2,1,0:T(8,128)(2,1)} broadcast(bf16[128,3072]{1,0:T(8,128)(2,1)} %bitcast.19), dimensions={2,3} | broadcast | bytes 7077888 | tf_op jit(solution)/shard_map/stack | solution.py:33
  204.1 0.0 copy-start.3
  204.1 0.0 copy-start.2
  204.1 0.0 copy-done.1
  204.1 5.1 %all-to-all-start.4 = ((bf16[8,1,128,3072]{3,2,1,0:T(8,128)(2,1)}), bf16[8,1,128,3072]{3,2,1,0:T(8,128)(2,1)}, u32[]{:S(2)}, u32[]{:S(2)}) async-start(bf16[8,1,128,3072]{3,2,1,0:T(8,128)(2,1)} %stack.8), calls=%async_computation.4 | async-start | bytes 12582912 | tf_op jit(solution)/shard_map/all_to_all | solution.py:34
  209.3 0.0 copy-done.3
  209.3 0.6 fusion.25
  213.4 0.0 copy-done.2
  213.5 0.1 broadcast_subtract_fusion
  213.5 0.3 reshape.221
  213.8 0.5 bitcast_convert_fusion.2
  214.4 0.3 copy.19
  214.7 0.1 reshape.214
  214.8 4.3 %convolution_add_fusion.2 = f32[128,3072]{1,0:T(8,128)S(1)} fusion(bf16[1024,3072]{1,0:T(8,128)(2,1)} %bitcast.2, f32[1,128,3072]{2,1,0:T(8,128)} %param.7, f32[1,1024,1,128]{1,3,2,0:T(8,128)S(1)} %reshape.214, bf16[128,1024]{1,0:T(8,128)(2,1)S(1)} %convolution_convert_fusion.2, f32[1024]{0:T(1024)S(1)} %copy-done.2, f32[128]{0:T(128)S(1)} %get-tuple-element.7), kind=kOutput, calls=%fused_computation.3 | convolution fusion | flops 806486016 | bytes 10228224 | tf_op jit(solution)/shard_map/dot_general | solution.py:55
  219.1 1.2 reshape.223
  220.3 0.5 bitcast_convert_fusion.1
  220.8 1.1 copy.18
  221.9 1.1 reshape.215
  223.1 53.0 %all-to-all-done.4 = bf16[8,1,128,3072]{3,2,1,0:T(8,128)(2,1)} async-done(((bf16[8,1,128,3072]{3,2,1,0:T(8,128)(2,1)}), bf16[8,1,128,3072]{3,2,1,0:T(8,128)(2,1)}, u32[]{:S(2)}, u32[]{:S(2)}) %all-to-all-start.4) | async-done | bytes 6291488 | tf_op jit(solution)/shard_map/all_to_all | solution.py:34
  276.0 5.0 %convolution_convert_fusion = bf16[128,1024]{1,0:T(8,128)(2,1)S(1)} fusion(bf16[1024,3072]{1,0:T(8,128)(2,1)} %bitcast.20, bf16[1,128,3072]{2,1,0:T(8,128)(2,1)S(1)} %copy-done), kind=kOutput, calls=%fused_computation.4 | convolution fusion | flops 805437440 | bytes 7340032 | tf_op jit(solution)/shard_map/dot_general | solution.py:39
  281.0 0.4 copy.12
  281.4 2.2 reduce.2
  283.6 0.8 reshape.224
  284.4 3.6 %all-to-all-start.5 = ((bf16[8,2,8192]{2,1,0:T(2,128)(2,1)}), bf16[8,2,8192]{2,1,0:T(2,128)(2,1)S(1)}, u32[]{:S(2)}, u32[]{:S(2)}) async-start(bf16[8,2,8192]{2,1,0:T(2,128)(2,1)} %reshape.224), calls=%async_computation.5 | async-start | bytes 524288 | tf_op jit(solution)/shard_map/all_to_all | solution.py:43
  288.0 5.0 %convolution_add_fusion.1 = f32[128,3072]{1,0:T(8,128)} fusion(f32[128,3072]{1,0:T(8,128)S(1)} %convolution_add_fusion.2, bf16[1024,3072]{1,0:T(8,128)(2,1)} %bitcast.11, f32[1,1024,1,128]{1,3,2,0:T(8,128)S(1)} %reshape.215, bf16[128,1024]{1,0:T(8,128)(2,1)S(1)} %convolution_convert_fusion.1, f32[128]{0:T(128)S(1)} %get-tuple-element.6, f32[1024]{0:T(1024)S(1)} %copy-done.2), kind=kOutput, calls=%fused_computation.2 | convolution fusion | flops 806486016 | bytes 10228224 | tf_op jit(solution)/shard_map/dot_general | solution.py:55
  293.0 2.4 all-to-all-done.5
  295.4 0.3 reshape.225
  295.6 0.5 bitcast_convert_fusion
  296.2 0.3 copy.17
  296.5 0.1 reshape.216
  296.6 5.5 %fusion = f32[1,128,3072]{2,1,0:T(8,128)} fusion(f32[128,3072]{1,0:T(8,128)} %convolution_add_fusion.1, bf16[1024,3072]{1,0:T(8,128)(2,1)} %bitcast.20, f32[1,1024,1,128]{1,3,2,0:T(8,128)S(1)} %reshape.216, bf16[128,1024]{1,0:T(8,128)(2,1)S(1)} %convolution_convert_fusion, f32[128]{0:T(128)S(1)} %get-tuple-element.5, f32[1024]{0:T(1024)S(1)} %copy-done.2), kind=kOutput, calls=%fused_computation.1 | convolution fusion | flops 806486016 | bytes 10228224 | tf_op jit(solution)/shard_map/dot_general | solution.py:55
Async XLA Ops:
  4.6 5.2 %copy-start = (bf16[1,128,3072]{2,1,0:T(8,128)(2,1)S(1)}, bf16[1,128,3072]{2,1,0:T(8,128)(2,1)}, u32[]{:S(2)}) copy-start(bf16[1,128,3072]{2,1,0:T(8,128)(2,1)} %param.4) | copy-start | bytes 2359300
  4.6 83.7 %all-to-all-start = ((bf16[8,1,128,3072]{3,2,1,0:T(8,128)(2,1)}), bf16[8,1,128,3072]{3,2,1,0:T(8,128)(2,1)}, u32[]{:S(2)}, u32[]{:S(2)}) async-start(bf16[8,1,128,3072]{3,2,1,0:T(8,128)(2,1)} %stack.6), calls=%async_computation | async-start | bytes 12582912 | tf_op jit(solution)/shard_map/all_to_all | solution.py:34
  9.9 77.3 %collective-permute-start = (bf16[1,128,3072]{2,1,0:T(8,128)(2,1)S(1)}, bf16[1,128,3072]{2,1,0:T(8,128)(2,1)S(1)}, u32[]{:S(2)}, u32[]{:S(2)}) collective-permute-start(bf16[1,128,3072]{2,1,0:T(8,128)(2,1)S(1)} %copy-done), channel_id=1, source_target_pairs={{248,0},{0,8},{8,16},{16,24},{24,32},{32,40},{40,48},{48,56},{56,6... | collective-permute-start | bytes 2359304 | tf_op jit(solution)/shard_map/ppermute | solution.py:12
  91.7 82.2 %all-to-all-start.2 = ((bf16[8,1,128,3072]{3,2,1,0:T(8,128)(2,1)}), bf16[8,1,128,3072]{3,2,1,0:T(8,128)(2,1)}, u32[]{:S(2)}, u32[]{:S(2)}) async-start(bf16[8,1,128,3072]{3,2,1,0:T(8,128)(2,1)} %stack.7), calls=%async_computation.2 | async-start | bytes 12582912 | tf_op jit(solution)/shard_map/all_to_all | solution.py:34
  96.7 95.6 %collective-permute-start.1 = (bf16[1,128,3072]{2,1,0:T(8,128)(2,1)S(1)}, bf16[1,128,3072]{2,1,0:T(8,128)(2,1)}, u32[]{:S(2)}, u32[]{:S(2)}) collective-permute-start(bf16[1,128,3072]{2,1,0:T(8,128)(2,1)S(1)} %collective-permute-done), channel_id=1, source_target_pairs={{248,0},{0,8},{8,16},{16,24},{24,32},{32,40},{40,48},{48,56},{56,6... | collective-permute-start | bytes 2359304 | tf_op jit(solution)/shard_map/ppermute | solution.py:12
  173.9 12.6 %all-to-all-start.1 = ((bf16[8,2,8192]{2,1,0:T(2,128)(2,1)}), bf16[8,2,8192]{2,1,0:T(2,128)(2,1)S(1)}, u32[]{:S(2)}, u32[]{:S(2)}) async-start(bf16[8,2,8192]{2,1,0:T(2,128)(2,1)} %reshape.220), calls=%async_computation.1 | async-start | bytes 524288 | tf_op jit(solution)/shard_map/all_to_all | solution.py:43
  186.5 12.9 %all-to-all-start.3 = ((bf16[8,2,8192]{2,1,0:T(2,128)(2,1)}), bf16[8,2,8192]{2,1,0:T(2,128)(2,1)S(1)}, u32[]{:S(2)}, u32[]{:S(2)}) async-start(bf16[8,2,8192]{2,1,0:T(2,128)(2,1)} %reshape.222), calls=%async_computation.3 | async-start | bytes 524288 | tf_op jit(solution)/shard_map/all_to_all | solution.py:43
  199.5 4.7 %copy-start.1 = (bf16[8,2,8192]{2,1,0:T(2,128)(2,1)}, bf16[8,2,8192]{2,1,0:T(2,128)(2,1)S(1)}, u32[]{:S(2)}) copy-start(bf16[8,2,8192]{2,1,0:T(2,128)(2,1)S(1)} %all-to-all-done.3) | copy-start | bytes 786436
  204.1 5.2 %copy-start.3 = (f32[32]{0:T(128)S(1)}, f32[32]{0:T(128)}, u32[]{:S(2)}) copy-start(f32[32]{0:T(128)} %param.5) | copy-start | bytes 388
  204.1 9.3 %copy-start.2 = (f32[1024]{0:T(1024)S(1)}, f32[1024]{0:T(1024)}, u32[]{:S(2)}) copy-start(f32[1024]{0:T(1024)} %param.6) | copy-start | bytes 12292
  204.1 71.9 %all-to-all-start.4 = ((bf16[8,1,128,3072]{3,2,1,0:T(8,128)(2,1)}), bf16[8,1,128,3072]{3,2,1,0:T(8,128)(2,1)}, u32[]{:S(2)}, u32[]{:S(2)}) async-start(bf16[8,1,128,3072]{3,2,1,0:T(8,128)(2,1)} %stack.8), calls=%async_computation.4 | async-start | bytes 12582912 | tf_op jit(solution)/shard_map/all_to_all | solution.py:34
  284.4 11.0 %all-to-all-start.5 = ((bf16[8,2,8192]{2,1,0:T(2,128)(2,1)}), bf16[8,2,8192]{2,1,0:T(2,128)(2,1)S(1)}, u32[]{:S(2)}, u32[]{:S(2)}) async-start(bf16[8,2,8192]{2,1,0:T(2,128)(2,1)} %reshape.224), calls=%async_computation.5 | async-start | bytes 524288 | tf_op jit(solution)/shard_map/all_to_all | solution.py:43
